TPU v7x, 32 devices: a whole 2x2x4 slice. The times are simulated.
32 devices in a mesh: fsdp: 4 (over x, core), ctx: 4 (over z), tp: 2 (over y).
Axes of the slice: x: 2, y: 2, z: 4, core: 2. Of those that a mesh axis runs over, the one named last changes fastest.
Arguments:
- layer_input: bfloat16 [4096, 2048], P(('fsdp', 'ctx', 'tp')), may hold values from -6 to 6
- cotangent: bfloat16 [4096, 2048], P(('fsdp', 'ctx', 'tp')), may hold values from -6 to 6
- lengths: int32 [4, 2], P('fsdp'), may hold values from 0 to 1024, as said below
- attn_norm: bfloat16 [2048], replicated, may hold values from 0.5 to 1.5
- query_norm_gain: bfloat16 [128], replicated, may hold values from 0.25 to 1.75
- k_norm: bfloat16 [128], replicated, may hold values from 0.25 to 1.75
- w_query: bfloat16 [2048, 2048], P('fsdp', 'tp'), may hold values from -0.125 to 0.125
- key_weight: bfloat16 [2048, 1024], P('fsdp', 'tp'), may hold values from -0.125 to 0.125
- value_weight: bfloat16 [2048, 1024], P('fsdp', 'tp'), may hold values from -0.125 to 0.125
- w_out_gate: bfloat16 [2048, 2048], P('fsdp', 'tp'), may hold values from -0.125 to 0.125
- w_output: bfloat16 [2048, 2048], P(('tp', 'fsdp')), may hold values from -2 to 2
- ffn_norm: bfloat16 [2048], replicated, may hold values from 0.5 to 1.5
- w_gate: bfloat16 [2048, 6144], P('fsdp', 'tp'), may hold values from -0.125 to 0.125
- w_up: bfloat16 [2048, 6144], P('fsdp', 'tp'), may hold values from -0.125 to 0.125
- w_down: bfloat16 [6144, 2048], P(('tp', 'fsdp')), may hold values from -0.078125 to 0.078125
Outputs:
- layer_output: bfloat16 [4096, 2048], P(('fsdp', 'ctx', 'tp'))
- input_grad: bfloat16 [4096, 2048], P(('fsdp', 'ctx', 'tp'))
- grad_attn_norm: float32 [2048], replicated
- grad_q_norm: float32 [128], replicated
- grad_k_norm: float32 [128], replicated
- grad_w_query: float32 [2048, 2048], P('fsdp', 'tp')
- grad_w_key: float32 [2048, 1024], P('fsdp', 'tp')
- grad_w_value: float32 [2048, 1024], P('fsdp', 'tp')
- grad_w_out_gate: float32 [2048, 2048], P('fsdp', 'tp')
- grad_w_output: float32 [2048, 2048], P(('tp', 'fsdp'))
- grad_ffn_norm: float32 [2048], replicated
- grad_w_gate: float32 [2048, 6144], P('fsdp', 'tp')
- grad_w_up: float32 [2048, 6144], P('fsdp', 'tp')
- grad_w_down: float32 [6144, 2048], P(('tp', 'fsdp'))
Inputs may be any that keep to these rules, and one draw needn't show every extreme that they name: `lengths`: per packed row the first count is at least 512 and the two counts add up to at most 1024; some row holds a single sequence of 1024 tokens.
All inputs are finite; a program needn't handle non-finite values.
Results may differ from a plain program's by a relative error of at most 0.024.
Values may be sent and summed in bfloat16 or wider, within the bound.
No kernel may reach another device: no remote copies, remote signals or barrier semaphores. Data moves between devices by JAX's collectives and lax.ppermute only.
A program may use at most 448 MiB of HBM per device.

v0:
```python
import jax
import jax.numpy as jnp
from jax import lax
from jax.sharding import PartitionSpec as P

HEAD_SIZE = 128
EPSILON = 1e-06
ROPE_BASE = 1000000.0
NEG_FILL = -1e30


def as_sent(value):

    def short(part):
        return part.astype(jnp.bfloat16) if part.dtype == jnp.float32 else part

    return jax.tree.map(short, value)


def apply_rms_norm(values, gain_vec):
    return (
        values * lax.rsqrt(jnp.mean(values * values, axis=-1, keepdims=True) + EPSILON) * gain_vec
    )


def norm_back(values, gain_vec, grad_in):
    row_scale = lax.rsqrt(jnp.mean(values * values, axis=-1, keepdims=True) + EPSILON)
    unit_rows = values * row_scale
    scaled = grad_in * gain_vec
    back_rows = row_scale * (
        scaled - unit_rows * jnp.mean(scaled * unit_rows, axis=-1, keepdims=True)
    )
    gain_grad = jnp.sum((grad_in * unit_rows).reshape(-1, values.shape[-1]), axis=0)
    return (back_rows, gain_grad)


def apply_rotary(values, token_position, direction):
    half_size = values.shape[-1] // 2
    frequency = jnp.power(ROPE_BASE, -jnp.arange(half_size, dtype=jnp.float32) / half_size)
    angle = token_position.astype(jnp.float32)[:, None] * frequency[None, :]
    cosine = jnp.cos(angle)[:, None, :]
    sine = direction * jnp.sin(angle)[:, None, :]
    first_half = values[..., :half_size]
    second_half = values[..., half_size:]
    return jnp.concatenate(
        [first_half * cosine - second_half * sine, second_half * cosine + first_half * sine],
        axis=-1,
    )


def segment_of(slot_ids, lengths):
    first_len = lengths[0, 0]
    second_len = lengths[0, 1]
    return jnp.where(slot_ids < first_len, 0, jnp.where(slot_ids < first_len + second_len, 1, 2))


def position_of(slot_ids, segment, lengths):
    seg_begin = jnp.where(
        segment == 0, 0, jnp.where(segment == 1, lengths[0, 0], lengths[0, 0] + lengths[0, 1])
    )
    return slot_ids - seg_begin


def to_block(local_part):
    return lax.all_gather(local_part, "tp", axis=0, tiled=True)


def to_share(partial_rows):
    return lax.psum_scatter(
        partial_rows.astype(jnp.bfloat16), "tp", scatter_dimension=0, tiled=True
    ).astype(jnp.float32)


def fold_product(left_rows, weight_set):
    pieces = jax.tree.map(
        lambda a: lax.all_gather(a, "fsdp", axis=0, tiled=True), as_sent(weight_set)
    )
    return tuple(
        (
            jnp.dot(left_rows, weight_part, preferred_element_type=jnp.float32)
            for weight_part in pieces
        )
    )


def back_product(grad_rows, weight_set):
    pieces = jax.tree.map(
        lambda a: lax.all_gather(a, "fsdp", axis=0, tiled=True), as_sent(weight_set)
    )
    result = lax.dot_general(
        grad_rows[0], pieces[0], (((1,), (1,)), ((), ())), preferred_element_type=jnp.float32
    )
    for grad_part, weight_part in zip(grad_rows[1:], pieces[1:]):
        result = result + lax.dot_general(
            grad_part, weight_part, (((1,), (1,)), ((), ())), preferred_element_type=jnp.float32
        )
    return result


def weight_grads(left_rows, grad_rows):
    widths = [grad_part.shape[1] for grad_part in grad_rows]
    shared = lax.psum_scatter(
        jnp.concatenate(
            [
                lax.dot_general(
                    left_rows,
                    grad_part,
                    (((0,), (0,)), ((), ())),
                    preferred_element_type=jnp.float32,
                )
                for grad_part in grad_rows
            ],
            axis=1,
        ).astype(jnp.bfloat16),
        "fsdp",
        scatter_dimension=0,
        tiled=True,
    )
    summed = lax.psum(shared, "ctx").astype(jnp.float32)
    pieces = []
    offset = 0
    for column_width in widths:
        pieces.append(summed[:, offset : offset + column_width])
        offset = offset + column_width
    return tuple(pieces)


def body(
    layer_input,
    cotangent,
    lengths,
    attn_norm,
    query_norm_gain,
    k_norm,
    w_query,
    key_weight,
    value_weight,
    w_out_gate,
    w_output,
    ffn_norm,
    w_gate,
    w_up,
    w_down,
):
    local_rows = layer_input.shape[0]
    block_rows = local_rows * lax.axis_size("tp")
    query_heads = w_query.shape[1] // HEAD_SIZE
    kv_heads = key_weight.shape[1] // HEAD_SIZE
    groups = query_heads // kv_heads
    score_scale = HEAD_SIZE ** (-0.5)
    block_first = lax.axis_index("ctx") * block_rows
    own_slots = (
        block_first + lax.axis_index("tp") * local_rows + jnp.arange(local_rows, dtype=jnp.int32)
    )
    own_valid = (segment_of(own_slots, lengths) < 2).astype(jnp.float32)[:, None]
    query_slots = block_first + jnp.arange(block_rows, dtype=jnp.int32)
    query_segment = segment_of(query_slots, lengths)
    query_position = position_of(query_slots, query_segment, lengths)
    inputs = layer_input.astype(jnp.float32)
    gain_one = attn_norm.astype(jnp.float32)
    gain_two = ffn_norm.astype(jnp.float32)
    query_gain = query_norm_gain.astype(jnp.float32)
    key_gain = k_norm.astype(jnp.float32)
    first_normed = to_block(apply_rms_norm(inputs, gain_one).astype(jnp.bfloat16))
    query_rows, key_projected, value_proj, gate_logits = fold_product(
        first_normed, (w_query, key_weight, value_weight, w_out_gate)
    )
    query_heads_raw = query_rows.reshape(block_rows, query_heads, HEAD_SIZE)
    key_heads_raw = key_projected.reshape(block_rows, kv_heads, HEAD_SIZE)
    query_rotated = apply_rotary(
        apply_rms_norm(query_heads_raw, query_gain), query_position, 1.0
    ).astype(jnp.bfloat16)
    key_rot = apply_rotary(apply_rms_norm(key_heads_raw, key_gain), query_position, 1.0).astype(
        jnp.bfloat16
    )
    query_grouped = query_rotated.reshape(block_rows, kv_heads, groups, HEAD_SIZE)
    key_flat = key_rot.reshape(block_rows, kv_heads * HEAD_SIZE)
    value_reduced = value_proj.astype(jnp.bfloat16)

    def key_mask(piece_rows):
        key_slots = jnp.arange(piece_rows, dtype=jnp.int32)
        key_segment = segment_of(key_slots, lengths)
        return (query_segment[:, None] == key_segment[None, :]) & (
            key_slots[None, :] <= query_slots[:, None]
        )

    head_shape = (kv_heads, groups, block_rows)
    running_top = jnp.full(head_shape + (1,), NEG_FILL, jnp.float32)
    key_piece = lax.all_gather(key_flat, "ctx", axis=0, tiled=True)
    value_piece = lax.all_gather(value_reduced, "ctx", axis=0, tiled=True)
    piece_rows = key_piece.shape[0]
    allowed = key_mask(piece_rows)
    raw_scores = jnp.einsum(
        "qhgd,khd->hgqk",
        query_grouped,
        key_piece.reshape(piece_rows, kv_heads, HEAD_SIZE),
        preferred_element_type=jnp.float32,
    )
    scores = jnp.where(allowed, raw_scores * score_scale, NEG_FILL)
    new_top = jnp.maximum(running_top, jnp.max(scores, axis=-1, keepdims=True))
    weights = jnp.where(allowed, jnp.exp(scores - new_top), 0.0)
    running_total = jnp.sum(weights, axis=-1, keepdims=True)
    mixed_sum = jnp.einsum(
        "hgqk,khd->hgqd",
        weights.astype(jnp.bfloat16),
        value_piece.reshape(piece_rows, kv_heads, HEAD_SIZE),
        preferred_element_type=jnp.float32,
    )
    mixed_sum, running_top, running_total = (mixed_sum, new_top, running_total)
    log_total = running_top + jnp.log(running_total)
    attended = jnp.transpose(mixed_sum / running_total, (2, 0, 1, 3))
    attended_rows = attended.reshape(block_rows, query_heads * HEAD_SIZE)
    gate_sig = jax.nn.sigmoid(gate_logits)
    gated_mix = (attended_rows * gate_sig).astype(jnp.bfloat16)
    attn_share = to_share(fold_product(gated_mix, (w_output,))[0])
    hidden_in = inputs + own_valid * attn_share
    normed_two = to_block(apply_rms_norm(hidden_in, gain_two).astype(jnp.bfloat16))
    gate_pre, up_pre = fold_product(normed_two, (w_gate, w_up))
    gate_sigmoid = jax.nn.sigmoid(gate_pre)
    activated = gate_pre * gate_sigmoid
    hidden_act = (activated * up_pre).astype(jnp.bfloat16)
    ffn_share = to_share(fold_product(hidden_act, (w_down,))[0])
    layer_output = (hidden_in + own_valid * ffn_share).astype(jnp.bfloat16)
    out_grad = cotangent.astype(jnp.float32) * own_valid
    ffn_grad = to_block(out_grad.astype(jnp.bfloat16))
    hidden_grad = back_product((ffn_grad,), (w_down,))
    grad_w_down = weight_grads(hidden_act, (ffn_grad,))[0]
    gate_grad = (
        hidden_grad * up_pre * gate_sigmoid * (1.0 + gate_pre * (1.0 - gate_sigmoid))
    ).astype(jnp.bfloat16)
    up_grad = (hidden_grad * activated).astype(jnp.bfloat16)
    normed_two_grad = to_share(back_product((gate_grad, up_grad), (w_gate, w_up)))
    grad_w_gate, grad_w_up = weight_grads(normed_two, (gate_grad, up_grad))
    back_two, gain_two_grad = norm_back(hidden_in, gain_two, normed_two_grad)
    hidden_total_grad = out_grad + back_two
    attn_grad = to_block((own_valid * hidden_total_grad).astype(jnp.bfloat16))
    gated_grad = back_product((attn_grad,), (w_output,))
    grad_w_output = weight_grads(gated_mix, (attn_grad,))[0]
    mixed_grad = (gated_grad * gate_sig).astype(jnp.bfloat16)
    gate_logit_grad = (gated_grad * attended_rows * gate_sig * (1.0 - gate_sig)).astype(
        jnp.bfloat16
    )
    mixed_grad_heads = mixed_grad.reshape(block_rows, kv_heads, groups, HEAD_SIZE)
    delta_rows = jnp.transpose(
        jnp.sum(mixed_grad_heads.astype(jnp.float32) * attended, axis=-1), (1, 2, 0)
    )[..., None]
    key_piece = lax.all_gather(key_flat, "ctx", axis=0, tiled=True)
    value_piece = lax.all_gather(value_reduced, "ctx", axis=0, tiled=True)
    piece_rows = key_piece.shape[0]
    key_view = key_piece.reshape(piece_rows, kv_heads, HEAD_SIZE)
    value_view = value_piece.reshape(piece_rows, kv_heads, HEAD_SIZE)
    allowed = key_mask(piece_rows)
    raw_scores = jnp.einsum(
        "qhgd,khd->hgqk", query_grouped, key_view, preferred_element_type=jnp.float32
    )
    soft_vals = jnp.where(allowed, jnp.exp(raw_scores * score_scale - log_total), 0.0)
    prob_grad = jnp.einsum(
        "qhgd,khd->hgqk", mixed_grad_heads, value_view, preferred_element_type=jnp.float32
    )
    score_grad = (soft_vals * (prob_grad - delta_rows) * score_scale).astype(jnp.bfloat16)
    query_acc = jnp.einsum(
        "hgqk,khd->qhgd", score_grad, key_view, preferred_element_type=jnp.float32
    )
    key_part = jnp.einsum(
        "hgqk,qhgd->khd", score_grad, query_grouped, preferred_element_type=jnp.float32
    ).reshape(piece_rows, kv_heads * HEAD_SIZE)
    value_part = jnp.einsum(
        "hgqk,qhgd->khd",
        soft_vals.astype(jnp.bfloat16),
        mixed_grad_heads,
        preferred_element_type=jnp.float32,
    ).reshape(piece_rows, kv_heads * HEAD_SIZE)
    kv_acc = jnp.concatenate([key_part, value_part], axis=1)
    query_acc, kv_acc = (query_acc, kv_acc)
    kv_own = lax.psum_scatter(
        kv_acc.astype(jnp.bfloat16), "ctx", scatter_dimension=0, tiled=True
    ).astype(jnp.float32)
    key_rot_grad = kv_own[:, : kv_heads * HEAD_SIZE].reshape(block_rows, kv_heads, HEAD_SIZE)
    value_grad = kv_own[:, kv_heads * HEAD_SIZE :].astype(jnp.bfloat16)
    key_back, key_gain_grad = norm_back(
        key_heads_raw, key_gain, apply_rotary(key_rot_grad, query_position, -1.0)
    )
    query_back, query_gain_grad = norm_back(
        query_heads_raw,
        query_gain,
        apply_rotary(query_acc.reshape(block_rows, query_heads, HEAD_SIZE), query_position, -1.0),
    )
    query_grad = query_back.reshape(block_rows, query_heads * HEAD_SIZE).astype(jnp.bfloat16)
    key_grad = key_back.reshape(block_rows, kv_heads * HEAD_SIZE).astype(jnp.bfloat16)
    attn_in_grads = (query_grad, key_grad, value_grad, gate_logit_grad)
    normed_one_grad = to_share(
        back_product(attn_in_grads, (w_query, key_weight, value_weight, w_out_gate))
    )
    grad_w_query, grad_w_key, grad_w_value, grad_w_out_gate = weight_grads(
        first_normed, attn_in_grads
    )
    back_one, gain_one_grad = norm_back(inputs, gain_one, normed_one_grad)
    input_grad = (hidden_total_grad + back_one).astype(jnp.bfloat16)
    gain_totals = lax.psum(
        (gain_one_grad, query_gain_grad, key_gain_grad, gain_two_grad), ("fsdp", "ctx", "tp")
    )
    return (
        layer_output,
        input_grad,
        gain_totals[0],
        gain_totals[1],
        gain_totals[2],
        grad_w_query,
        grad_w_key,
        grad_w_value,
        grad_w_out_gate,
        grad_w_output,
        gain_totals[3],
        grad_w_gate,
        grad_w_up,
        grad_w_down,
    )


def solution(mesh):
    return jax.shard_map(
        body,
        mesh=mesh,
        in_specs=(
            P(("fsdp", "ctx", "tp"), None),
            P(("fsdp", "ctx", "tp"), None),
            P("fsdp", None),
            P(),
            P(),
            P(),
            P("fsdp", "tp"),
            P("fsdp", "tp"),
            P("fsdp", "tp"),
            P("fsdp", "tp"),
            P(("tp", "fsdp"), None),
            P(),
            P("fsdp", "tp"),
            P("fsdp", "tp"),
            P(("tp", "fsdp"), None),
        ),
        out_specs=(
            P(("fsdp", "ctx", "tp"), None),
            P(("fsdp", "ctx", "tp"), None),
            P(),
            P(),
            P(),
            P("fsdp", "tp"),
            P("fsdp", "tp"),
            P("fsdp", "tp"),
            P("fsdp", "tp"),
            P(("tp", "fsdp"), None),
            P(),
            P("fsdp", "tp"),
            P("fsdp", "tp"),
            P(("tp", "fsdp"), None),
        ),
        check_vma=False,
    )
```

profile of v0, /device:TPU:0, one launch (start us, length us, event | category | flops | bytes accessed | tf_op | source)
XLA Modules:
  0.0 1699.3 jit_solution(15141842273888128146)
XLA Ops:
  12.8 22.6 %all-gather.15.cloned.1.call-done = bf16[256,2048]{1,0:T(8,128)(2,1)} async-done(((bf16[128,2048]{1,0:T(8,128)(2,1)}), bf16[256,2048]{1,0:T(8,128)(2,1)}) %all-gather.15.cloned.1.call-update) | async-done | bytes 1048592 | tf_op jit(solution)/shard_map/all_gather | solution.py:65
  35.4 24.1 %all-gather.23.cloned.1.call-done = bf16[2048,512]{1,0:T(8,128)(2,1)} async-done(((bf16[512,512]{1,0:T(8,128)(2,1)}), bf16[2048,512]{1,0:T(8,128)(2,1)}) %all-gather.23.cloned.1.call-update) | async-done | bytes 2097168 | tf_op jit(solution)/shard_map/all_gather | solution.py:76
  67.3 16.4 all-gather.17.cloned.1.call-done
  92.2 21.5 %all-gather.25.cloned.1.call-done = bf16[1024,512]{1,0:T(8,128)(2,1)} async-done(((bf16[256,512]{1,0:T(8,128)(2,1)}), bf16[1024,512]{1,0:T(8,128)(2,1)}) %all-gather.25.cloned.1.call-update) | async-done | bytes 1048592 | tf_op jit(solution)/shard_map/all_gather | solution.py:190
  115.9 33.1 %all-gather.21.cloned.1.call-done = bf16[2048,1024]{1,0:T(8,128)(2,1)} async-done(((bf16[512,1024]{1,0:T(8,128)(2,1)}), bf16[2048,1024]{1,0:T(8,128)(2,1)}) %all-gather.21.cloned.1.call-update) | async-done | bytes 4194320 | tf_op jit(solution)/shard_map/all_gather | solution.py:76
  155.1 25.9 %all-gather.19.cloned.1.call-done = bf16[1024,512]{0,1:T(8,128)(2,1)} async-done(((bf16[256,512]{0,1:T(8,128)(2,1)}), bf16[1024,512]{0,1:T(8,128)(2,1)}) %all-gather.19.cloned.1.call-update) | async-done | bytes 1048592 | tf_op jit(solution)/shard_map/all_gather | solution.py:189
  193.8 21.5 %all-gather.27.cloned.1.call-done = bf16[2048,1024]{1,0:T(8,128)(2,1)} async-done(((bf16[512,1024]{1,0:T(8,128)(2,1)}), bf16[2048,1024]{1,0:T(8,128)(2,1)}) %all-gather.27.cloned.1.call-update) | async-done | bytes 4194320 | tf_op jit(solution)/shard_map/all_gather | solution.py:76
  220.3 31.1 %all-gather.29.cloned.1.call-done = bf16[1024,2048]{1,0:T(8,128)(2,1)} async-done(((bf16[256,2048]{1,0:T(8,128)(2,1)}), bf16[1024,2048]{1,0:T(8,128)(2,1)}) %all-gather.29.cloned.1.call-update) | async-done | bytes 4194320 | tf_op jit(solution)/shard_map/all_gather | solution.py:76
  258.0 18.6 %reduce-scatter.10.cloned.1.call-done = bf16[128,2048]{1,0:T(8,128)(2,1)} async-done(((bf16[256,2048]{1,0:T(8,128)(2,1)}), bf16[128,2048]{1,0:T(8,128)(2,1)}) %reduce-scatter.10.cloned.1.call-update) | async-done | bytes 524304 | tf_op jit(solution)/shard_map/reduce_scatter | solution.py:69
  283.6 18.2 %all-gather.31.cloned.1.call-done = bf16[256,2048]{1,0:T(8,128)(2,1)} async-done(((bf16[128,2048]{1,0:T(8,128)(2,1)}), bf16[256,2048]{1,0:T(8,128)(2,1)}) %all-gather.31.cloned.1.call-update) | async-done | bytes 1048592 | tf_op jit(solution)/shard_map/all_gather | solution.py:65
  301.8 83.7 %all-gather.33.cloned.1.call-done = bf16[2048,3072]{1,0:T(8,128)(2,1)} async-done(((bf16[512,3072]{1,0:T(8,128)(2,1)}), bf16[2048,3072]{1,0:T(8,128)(2,1)}) %all-gather.33.cloned.1.call-update) | async-done | bytes 12582928 | tf_op jit(solution)/shard_map/all_gather | solution.py:76
  395.4 73.5 %all-gather.35.cloned.1.call-done = bf16[2048,3072]{1,0:T(8,128)(2,1)} async-done(((bf16[512,3072]{1,0:T(8,128)(2,1)}), bf16[2048,3072]{1,0:T(8,128)(2,1)}) %all-gather.35.cloned.1.call-update) | async-done | bytes 12582928 | tf_op jit(solution)/shard_map/all_gather | solution.py:76
  479.0 13.4 all-gather.39.cloned.1.call-done
  492.4 83.6 %all-gather.37.cloned.1.call-done = bf16[3072,2048]{1,0:T(8,128)(2,1)} async-done(((bf16[768,2048]{1,0:T(8,128)(2,1)}), bf16[3072,2048]{1,0:T(8,128)(2,1)}) %all-gather.37.cloned.1.call-update) | async-done | bytes 12582928 | tf_op jit(solution)/shard_map/all_gather | solution.py:76
  605.7 20.5 %reduce-scatter.14.cloned.1.call-done = bf16[128,2048]{1,0:T(8,128)(2,1)} async-done(((bf16[256,2048]{1,0:T(8,128)(2,1)}), bf16[128,2048]{1,0:T(8,128)(2,1)}) %reduce-scatter.14.cloned.1.call-update) | async-done | bytes 524304 | tf_op jit(solution)/shard_map/reduce_scatter | solution.py:69
  632.8 20.1 %all-gather.41.cloned.1.call-done = bf16[256,2048]{1,0:T(8,128)(2,1)} async-done(((bf16[128,2048]{1,0:T(8,128)(2,1)}), bf16[256,2048]{1,0:T(8,128)(2,1)}) %all-gather.41.cloned.1.call-update) | async-done | bytes 1048592 | tf_op jit(solution)/shard_map/all_gather | solution.py:65
  734.8 29.6 %pad_maximum_fusion.1 = bf16[2048,3072]{0,1:T(8,128)(2,1)} fusion(bf16[2048,1024]{0,1:T(8,128)(2,1)S(1)} %copy-done.3, bf16[2048,512]{0,1:T(8,128)(2,1)S(1)} %convolution_convert_fusion.6, bf16[2048,512]{0,1:T(8,128)(2,1)S(1)} %convolution_convert_fusion.7, bf16[2048,1024]{0,1:T(8,128)(2,1)S(1)} %copy-done.4), kind=kLoop, calls=%fused_computation.1 | loop fusion | flops 50331648 | bytes 25165824 | tf_op jit(solution)/shard_map/concatenate | solution.py:103
  782.0 20.1 %pad_maximum_fusion = bf16[2048,6144]{1,0:T(8,128)(2,1)} fusion(bf16[2048,3072]{1,0:T(8,128)(2,1)} %convolution_convert_fusion.1, bf16[2048,3072]{1,0:T(8,128)(2,1)} %convolution_convert_fusion.2), kind=kLoop, calls=%fused_computation | loop fusion | flops 50331648 | bytes 50331648 | tf_op jit(solution)/shard_map/concatenate | solution.py:103
  821.7 49.5 %reduce-scatter.26.cloned.1.call-done = bf16[768,2048]{1,0:T(8,128)(2,1)} async-done(((bf16[3072,2048]{1,0:T(8,128)(2,1)}), bf16[768,2048]{1,0:T(8,128)(2,1)}) %reduce-scatter.26.cloned.1.call-update) | async-done | bytes 3145744 | tf_op jit(solution)/shard_map/reduce_scatter | solution.py:102
  871.2 99.6 %reduce-scatter.20.cloned.1.call-done = bf16[512,3072]{0,1:T(8,128)(2,1)} async-done(((bf16[2048,3072]{0,1:T(8,128)(2,1)}), bf16[512,3072]{0,1:T(8,128)(2,1)}) %reduce-scatter.20.cloned.1.call-update) | async-done | bytes 3145744 | tf_op jit(solution)/shard_map/reduce_scatter | solution.py:102
  970.8 184.5 %reduce-scatter.24.cloned.1.call-done = bf16[512,6144]{1,0:T(8,128)(2,1)} async-done(((bf16[2048,6144]{1,0:T(8,128)(2,1)}), bf16[512,6144]{1,0:T(8,128)(2,1)}) %reduce-scatter.24.cloned.1.call-update) | async-done | bytes 6291472 | tf_op jit(solution)/shard_map/reduce_scatter | solution.py:102
  1163.6 15.0 reduce-scatter.18.cloned.1.call-done
  1180.1 40.4 %all-reduce = (f32[2048]{0:T(1024)}, f32[128]{0:T(128)}, f32[128]{0:T(128)}, f32[2048]{0:T(1024)}) all-reduce(f32[2048]{0:T(1024)S(1)} %get-tuple-element.44, f32[128]{0:T(128)S(1)} %fusion.51, f32[128]{0:T(128)S(1)} %fusion.62, f32[2048]{0:T(1024)S(1)} %copy-done.46), channel_id=1, replica_groups=mesh['fsdp'=4,'ctx'=4,'tp'=2] {'fsdp','ctx','tp'}, use_global_device_ids=true, to_apply=%region_17.18 | all-reduce | flops 4352 | bytes 34816 | tf_op jit(solution)/shard_map/psum | solution.py:299
  1223.9 440.9 %all-reduce.4.cloned.1.call-done = (bf16[512,3072]{0,1:T(8,128)(2,1)}, bf16[512,6144]{1,0:T(8,128)(2,1)}, bf16[256,2048]{1,0:T(8,128)(2,1)}, bf16[768,2048]{1,0:T(8,128)(2,1)}) async-done(((bf16[512,3072]{0,1:T(8,128)(2,1)}, bf16[512,6144]{1,0:T(8,128)(2,1)}, bf16[256,2048]{1,0:T(8,128)(2,1)}, bf16[768,2048]{1,0:T(8,128)(2,1)}), (bf16[512,3072]{0,1:T(8,128)(2,1)}, bf16[512,6144]{1,0:T(8,128)(2,1)}, ...) | async-done | bytes 13631504 | tf_op jit(solution)/shard_map/psum | solution.py:119
  (293 shorter events, 274.9 us)
Async XLA Ops:
  7.2 28.2 %all-gather.15.cloned.1.call-start = ((), (), s32[]{:S(2)}) async-start(), calls=%async_computation.9 | async-start | bytes 1572864 | tf_op jit(solution)/shard_map/all_gather | solution.py:65
  11.2 48.3 %all-gather.23.cloned.1.call-start = ((), (), s32[]{:S(2)}) async-start(), calls=%async_computation.13 | async-start | bytes 2621440 | tf_op jit(solution)/shard_map/all_gather | solution.py:76
  12.0 71.7 %all-gather.17.cloned.1.call-start = ((), (), s32[]{:S(2)}) async-start(), calls=%async_computation.10 | async-start | bytes 2621440 | tf_op jit(solution)/shard_map/all_gather | solution.py:76
  12.7 101.0 %all-gather.25.cloned.1.call-start = ((), (), s32[]{:S(2)}) async-start(), calls=%async_computation.14 | async-start | bytes 1310720 | tf_op jit(solution)/shard_map/all_gather | solution.py:190
  62.9 86.1 %all-gather.21.cloned.1.call-start = ((), (), s32[]{:S(2)}) async-start(), calls=%async_computation.12 | async-start | bytes 5242880 | tf_op jit(solution)/shard_map/all_gather | solution.py:76
  63.5 117.5 %all-gather.19.cloned.1.call-start = ((), (), s32[]{:S(2)}) async-start(), calls=%async_computation.11 | async-start | bytes 1310720 | tf_op jit(solution)/shard_map/all_gather | solution.py:189
  88.8 126.6 %all-gather.27.cloned.1.call-start = ((), (), s32[]{:S(2)}) async-start(), calls=%async_computation.15 | async-start | bytes 5242880 | tf_op jit(solution)/shard_map/all_gather | solution.py:76
  89.5 161.9 %all-gather.29.cloned.1.call-start = ((), (), s32[]{:S(2)}) async-start(), calls=%async_computation.16 | async-start | bytes 5242880 | tf_op jit(solution)/shard_map/all_gather | solution.py:76
  90.3 186.3 %reduce-scatter.10.cloned.1.call-start = ((), (), s32[]{:S(2)}) async-start(), calls=%async_computation.17 | async-start | bytes 1572864 | tf_op jit(solution)/shard_map/reduce_scatter | solution.py:69
  256.0 45.8 %all-gather.31.cloned.1.call-start = ((), (), s32[]{:S(2)}) async-start(), calls=%async_computation.18 | async-start | bytes 1572864 | tf_op jit(solution)/shard_map/all_gather | solution.py:65
  280.4 105.1 %all-gather.33.cloned.1.call-start = ((), (), s32[]{:S(2)}) async-start(), calls=%async_computation.19 | async-start | bytes 15728640 | tf_op jit(solution)/shard_map/all_gather | solution.py:76
  281.1 187.9 %all-gather.35.cloned.1.call-start = ((), (), s32[]{:S(2)}) async-start(), calls=%async_computation.20 | async-start | bytes 15728640 | tf_op jit(solution)/shard_map/all_gather | solution.py:76
  281.7 210.7 %all-gather.39.cloned.1.call-start = ((), (), s32[]{:S(2)}) async-start(), calls=%async_computation.23 | async-start | bytes 1572864 | tf_op jit(solution)/shard_map/all_gather | solution.py:65
  282.4 293.6 %all-gather.37.cloned.1.call-start = ((), (), s32[]{:S(2)}) async-start(), calls=%async_computation.21 | async-start | bytes 15728640 | tf_op jit(solution)/shard_map/all_gather | solution.py:76
  283.0 343.2 %reduce-scatter.14.cloned.1.call-start = ((), (), s32[]{:S(2)}) async-start(), calls=%async_computation.24 | async-start | bytes 1572864 | tf_op jit(solution)/shard_map/reduce_scatter | solution.py:69
  605.6 47.3 %all-gather.41.cloned.1.call-start = ((), (), s32[]{:S(2)}) async-start(), calls=%async_computation.25 | async-start | bytes 1572864 | tf_op jit(solution)/shard_map/all_gather | solution.py:65
  631.5 90.7 %reduce-scatter.16.cloned.1.call-start = ((), (), s32[]{:S(2)}) async-start(), calls=%async_computation.26 | async-start | bytes 2621440 | tf_op jit(solution)/shard_map/reduce_scatter | solution.py:275
  678.4 143.3 %reduce-scatter.22.cloned.1.call-start = ((), (), s32[]{:S(2)}) async-start(), calls=%async_computation.29 | async-start | bytes 5242880 | tf_op jit(solution)/shard_map/reduce_scatter | solution.py:102
  683.1 188.0 %reduce-scatter.26.cloned.1.call-start = ((), (), s32[]{:S(2)}) async-start(), calls=%async_computation.31 | async-start | bytes 15728640 | tf_op jit(solution)/shard_map/reduce_scatter | solution.py:102
  693.3 277.5 %reduce-scatter.20.cloned.1.call-start = ((), (), s32[]{:S(2)}) async-start(), calls=%async_computation.28 | async-start | bytes 15728640 | tf_op jit(solution)/shard_map/reduce_scatter | solution.py:102
  764.4 390.9 %reduce-scatter.24.cloned.1.call-start = ((), (), s32[]{:S(2)}) async-start(), calls=%async_computation.30 | async-start | bytes 31457280 | tf_op jit(solution)/shard_map/reduce_scatter | solution.py:102
  802.1 376.5 %reduce-scatter.18.cloned.1.call-start = ((), (), s32[]{:S(2)}) async-start(), calls=%async_computation.27 | async-start | bytes 1572864 | tf_op jit(solution)/shard_map/reduce_scatter | solution.py:69
  811.8 408.6 %reduce-scatter.12.cloned.1.call-start = ((), (), s32[]{:S(2)}) async-start(), calls=%async_computation.22 | async-start | bytes 1572864 | tf_op jit(solution)/shard_map/reduce_scatter | solution.py:69
  821.6 843.2 %all-reduce.4.cloned.1.call-start = ((), (), s32[]{:S(2)}) async-start(), calls=%async_computation.32 | async-start | bytes 27262976 | tf_op jit(solution)/shard_map/psum | solution.py:119
  (65 other events, 996.5 us)
Sparse Core Ops, SparseCore 0:
  11.4 23.9 all-gather.14
  37.0 22.5 all-gather.22
  61.1 22.5 all-gather.16
  85.7 27.9 all-gather.24
  115.2 33.8 all-gather.20
  151.0 29.9 all-gather.18
  182.5 32.7 all-gather.26
  216.9 34.4 all-gather.28
  256.1 20.3 reduce-scatter.9
  280.5 21.2 all-gather.30
  303.4 82.0 all-gather.32
  386.9 82.0 all-gather.34
  471.1 21.2 all-gather.38
  493.8 82.1 all-gather.36
  605.7 20.3 reduce-scatter.13
  631.6 21.2 all-gather.40
  678.5 43.6 reduce-scatter.15
  725.1 43.7 reduce-scatter.21
  771.5 99.6 reduce-scatter.25
  873.6 97.1 reduce-scatter.19
  973.4 181.8 reduce-scatter.23
  1158.1 20.3 reduce-scatter.17
  1181.4 20.5 reduce-scatter.11
  1204.8 459.9 all-reduce.3
where the time goes:
time: 1700 us
  waiting for transfers between devices  1330 us (78%)
  matrix products  153 us (9%)
  other arithmetic  98.6 us (6%)
  local copies, waits for them, and re-layouts  58.1 us (3%)
  blocking collectives  40.4 us (2%)
    psum x1, waiting for transfers between devices, weight_grads(): summed = lax.psum(shared, 'ctx').astype(jnp.float32)  441 us
    all_gather x8, waiting for transfers between devices, fold_product(): lax.all_gather(a, 'fsdp', axis=0, tiled=True)  367 us
    reduce_scatter x4, waiting for transfers between devices, weight_grads(): lax.psum_scatter(jnp.concatenate([lax.dot_general(left_rows, grad_part, (...  334 us
    all_gather x4, waiting for transfers between devices, to_block(): return lax.all_gather(local_part, 'tp', axis=0, tiled=True)  74.3 us
    reduce_scatter x4, waiting for transfers between devices, to_share(): lax.psum_scatter(partial_rows.astype(jnp.bfloat16), 'tp', scatter_dimensi...  54.1 us
    concatenate x2, other arithmetic, weight_grads(): jnp.concatenate([lax.dot_general(left_rows, grad_part, (((0,), (0,)), (()...  49.7 us
    dot_general x8, matrix products, fold_product(): jnp.dot(left_rows, weight_part, preferred_element_type=jnp.float32)  48.3 us
    psum x1, blocking collectives, body(): lax.psum((gain_one_grad, query_gain_grad, key_gain_grad, gain_two_grad),...  40.4 us
  transfers between devices with their start and end apart: 24, of which 22 were waited for; matrix products, arithmetic and copies ran while one was open for 12% of the time, Pallas kernels for 0%

commit v1 on v0

--- a/solution.py
+++ b/solution.py
@@ -7,6 +7,18 @@
 EPSILON = 1e-06
 ROPE_BASE = 1000000.0
 NEG_FILL = -1e30
+
+
+def doubled_up(x, axis, dim):
+    ways, here = (lax.axis_size(axis), lax.axis_index(axis))
+    grown, reach = (x, 1)
+    while reach < ways:
+        theirs = lax.ppermute(grown, axis, [(d, d ^ reach) for d in range(ways)])
+        mine_first = jnp.concatenate([grown, theirs], axis=dim)
+        theirs_first = jnp.concatenate([theirs, grown], axis=dim)
+        grown = jnp.where(here & reach == 0, mine_first, theirs_first)
+        reach = 2 * reach
+    return grown
 
 
 def as_sent(value):
@@ -62,7 +74,7 @@
 
 
 def to_block(local_part):
-    return lax.all_gather(local_part, "tp", axis=0, tiled=True)
+    return doubled_up(local_part, "tp", 0)
 
 
 def to_share(partial_rows):

time: 1700 us -> 1620 us (0.953)
  waiting for transfers between devices: 1330 us -> 1250 us
    all_gather x4 -> x0, waiting for transfers between devices: 74.3 us -> none  [to_block(): return lax.all_gather(local_part, 'tp', axis=0, tiled=True)]
    all_gather x8, waiting for transfers between devices: 367 us -> 321 us  [fold_product(): lax.all_gather(a, 'fsdp', axis=0, tiled=True)]
    ppermute x0 -> x4, waiting for transfers between devices: none -> 37.3 us  [doubled_up(): theirs = lax.ppermute(grown, axis, [(d, d ^ reach) for d in range(ways)])]
  transfers between devices with their start and end apart: 24 -> 24, of which waited for: 22 -> 21; matrix products, arithmetic and copies ran while one was open for 12% -> 13% of each run, Pallas kernels for 0% -> 0%
where the time goes in v1:
time: 1620 us
  waiting for transfers between devices  1250 us (77%)
  matrix products  158 us (10%)
  other arithmetic  92.2 us (6%)
  local copies, waits for them, and re-layouts  55.5 us (3%)
  blocking collectives  40.4 us (2%)
  between operations  17.2 us (1%)
    psum x1, waiting for transfers between devices, weight_grads(): summed = lax.psum(shared, 'ctx').astype(jnp.float32)  441 us
    reduce_scatter x4, waiting for transfers between devices, weight_grads(): lax.psum_scatter(jnp.concatenate([lax.dot_general(left_rows, grad_part, (...  330 us
    all_gather x8, waiting for transfers between devices, fold_product(): lax.all_gather(a, 'fsdp', axis=0, tiled=True)  321 us
    reduce_scatter x4, waiting for transfers between devices, to_share(): lax.psum_scatter(partial_rows.astype(jnp.bfloat16), 'tp', scatter_dimensi...  53.1 us
    dot_general x8, matrix products, fold_product(): jnp.dot(left_rows, weight_part, preferred_element_type=jnp.float32)  48.3 us
    concatenate x2, other arithmetic, weight_grads(): jnp.concatenate([lax.dot_general(left_rows, grad_part, (((0,), (0,)), (()...  48 us
    dot_general x8, matrix products, weight_grads(): lax.dot_general(left_rows, grad_part, (((0,), (0,)), ((), ())), preferred...  44.6 us
    psum x1, blocking collectives, body(): lax.psum((gain_one_grad, query_gain_grad, key_gain_grad, gain_two_grad),...  40.4 us
  transfers between devices with their start and end apart: 24, of which 21 were waited for; matrix products, arithmetic and copies ran while one was open for 13% of the time, Pallas kernels for 0%

profile of v1, /device:TPU:0, one launch (start us, length us, event | category | flops | bytes accessed | tf_op | source)
XLA Modules:
  0.0 1615.5 jit_solution(14347022326201853339)
XLA Ops:
  15.0 11.9 collective-permute-done
  42.3 16.8 %all-gather.11.cloned.1.call-done = bf16[2048,512]{1,0:T(8,128)(2,1)} async-done(((bf16[512,512]{1,0:T(8,128)(2,1)}), bf16[2048,512]{1,0:T(8,128)(2,1)}) %all-gather.11.cloned.1.call-update) | async-done | bytes 2097168 | tf_op jit(solution)/shard_map/all_gather | solution.py:88
  67.7 21.6 %all-gather.19.cloned.1.call-done = bf16[1024,512]{1,0:T(8,128)(2,1)} async-done(((bf16[256,512]{1,0:T(8,128)(2,1)}), bf16[1024,512]{1,0:T(8,128)(2,1)}) %all-gather.19.cloned.1.call-update) | async-done | bytes 1048592 | tf_op jit(solution)/shard_map/all_gather | solution.py:202
  91.5 33.1 %all-gather.15.cloned.1.call-done = bf16[2048,1024]{1,0:T(8,128)(2,1)} async-done(((bf16[512,1024]{1,0:T(8,128)(2,1)}), bf16[2048,1024]{1,0:T(8,128)(2,1)}) %all-gather.15.cloned.1.call-update) | async-done | bytes 4194320 | tf_op jit(solution)/shard_map/all_gather | solution.py:88
  130.0 26.5 %all-gather.13.cloned.1.call-done = bf16[1024,512]{0,1:T(8,128)(2,1)} async-done(((bf16[256,512]{0,1:T(8,128)(2,1)}), bf16[1024,512]{0,1:T(8,128)(2,1)}) %all-gather.13.cloned.1.call-update) | async-done | bytes 1048592 | tf_op jit(solution)/shard_map/all_gather | solution.py:201
  169.4 21.4 %all-gather.21.cloned.1.call-done = bf16[2048,1024]{1,0:T(8,128)(2,1)} async-done(((bf16[512,1024]{1,0:T(8,128)(2,1)}), bf16[2048,1024]{1,0:T(8,128)(2,1)}) %all-gather.21.cloned.1.call-update) | async-done | bytes 4194320 | tf_op jit(solution)/shard_map/all_gather | solution.py:88
  195.8 30.9 %all-gather.23.cloned.1.call-done = bf16[1024,2048]{1,0:T(8,128)(2,1)} async-done(((bf16[256,2048]{1,0:T(8,128)(2,1)}), bf16[1024,2048]{1,0:T(8,128)(2,1)}) %all-gather.23.cloned.1.call-update) | async-done | bytes 4194320 | tf_op jit(solution)/shard_map/all_gather | solution.py:88
  235.4 16.4 %reduce-scatter.10.cloned.1.call-done = bf16[128,2048]{1,0:T(8,128)(2,1)} async-done(((bf16[256,2048]{1,0:T(8,128)(2,1)}), bf16[128,2048]{1,0:T(8,128)(2,1)}) %reduce-scatter.10.cloned.1.call-update) | async-done | bytes 524304 | tf_op jit(solution)/shard_map/reduce_scatter | solution.py:81
  258.3 12.9 collective-permute-done.1
  271.2 64.3 %all-gather.25.cloned.1.call-done = bf16[2048,3072]{1,0:T(8,128)(2,1)} async-done(((bf16[512,3072]{1,0:T(8,128)(2,1)}), bf16[2048,3072]{1,0:T(8,128)(2,1)}) %all-gather.25.cloned.1.call-update) | async-done | bytes 12582928 | tf_op jit(solution)/shard_map/all_gather | solution.py:88
  345.7 73.2 %all-gather.27.cloned.1.call-done = bf16[2048,3072]{1,0:T(8,128)(2,1)} async-done(((bf16[512,3072]{1,0:T(8,128)(2,1)}), bf16[2048,3072]{1,0:T(8,128)(2,1)}) %all-gather.27.cloned.1.call-update) | async-done | bytes 12582928 | tf_op jit(solution)/shard_map/all_gather | solution.py:88
  428.9 73.7 %all-gather.29.cloned.1.call-done = bf16[3072,2048]{1,0:T(8,128)(2,1)} async-done(((bf16[768,2048]{1,0:T(8,128)(2,1)}), bf16[3072,2048]{1,0:T(8,128)(2,1)}) %all-gather.29.cloned.1.call-update) | async-done | bytes 12582928 | tf_op jit(solution)/shard_map/all_gather | solution.py:88
  502.6 13.8 multiply_convert_fusion
  532.8 20.5 %reduce-scatter.14.cloned.1.call-done = bf16[128,2048]{1,0:T(8,128)(2,1)} async-done(((bf16[256,2048]{1,0:T(8,128)(2,1)}), bf16[128,2048]{1,0:T(8,128)(2,1)}) %reduce-scatter.14.cloned.1.call-update) | async-done | bytes 524304 | tf_op jit(solution)/shard_map/reduce_scatter | solution.py:81
  558.4 12.5 collective-permute-done.3
  651.4 29.4 %pad_maximum_fusion.1 = bf16[2048,3072]{0,1:T(8,128)(2,1)} fusion(bf16[2048,1024]{0,1:T(8,128)(2,1)S(1)} %copy-done.22, bf16[2048,512]{0,1:T(8,128)(2,1)S(1)} %convolution_convert_fusion.6, bf16[2048,512]{0,1:T(8,128)(2,1)S(1)} %convolution_convert_fusion.7, bf16[2048,1024]{0,1:T(8,128)(2,1)S(1)} %copy-done.23), kind=kLoop, calls=%fused_computation.1 | loop fusion | flops 50331648 | bytes 25165824 | tf_op jit(solution)/shard_map/concatenate | solution.py:115
  691.8 11.6 convolution_convert_fusion.2
  703.4 18.6 %pad_maximum_fusion = bf16[2048,6144]{1,0:T(8,128)(2,1)} fusion(bf16[2048,3072]{1,0:T(8,128)(2,1)} %convolution_convert_fusion.1, bf16[2048,3072]{1,0:T(8,128)(2,1)} %convolution_convert_fusion.2), kind=kLoop, calls=%fused_computation | loop fusion | flops 50331648 | bytes 50331648 | tf_op jit(solution)/shard_map/concatenate | solution.py:115
  741.0 46.0 %reduce-scatter.26.cloned.1.call-done = bf16[768,2048]{1,0:T(8,128)(2,1)} async-done(((bf16[3072,2048]{1,0:T(8,128)(2,1)}), bf16[768,2048]{1,0:T(8,128)(2,1)}) %reduce-scatter.26.cloned.1.call-update) | async-done | bytes 3145744 | tf_op jit(solution)/shard_map/reduce_scatter | solution.py:114
  786.9 99.6 %reduce-scatter.20.cloned.1.call-done = bf16[512,3072]{0,1:T(8,128)(2,1)} async-done(((bf16[2048,3072]{0,1:T(8,128)(2,1)}), bf16[512,3072]{0,1:T(8,128)(2,1)}) %reduce-scatter.20.cloned.1.call-update) | async-done | bytes 3145744 | tf_op jit(solution)/shard_map/reduce_scatter | solution.py:114
  886.5 184.4 %reduce-scatter.24.cloned.1.call-done = bf16[512,6144]{1,0:T(8,128)(2,1)} async-done(((bf16[2048,6144]{1,0:T(8,128)(2,1)}), bf16[512,6144]{1,0:T(8,128)(2,1)}) %reduce-scatter.24.cloned.1.call-update) | async-done | bytes 6291472 | tf_op jit(solution)/shard_map/reduce_scatter | solution.py:114
  1077.9 16.1 reduce-scatter.18.cloned.1.call-done
  1095.5 40.4 %all-reduce = (f32[2048]{0:T(1024)}, f32[128]{0:T(128)}, f32[128]{0:T(128)}, f32[2048]{0:T(1024)}) all-reduce(f32[2048]{0:T(1024)S(1)} %get-tuple-element.44, f32[128]{0:T(128)S(1)} %fusion.51, f32[128]{0:T(128)S(1)} %fusion.62, f32[2048]{0:T(1024)S(1)} %copy-done.53), channel_id=1, replica_groups=mesh['fsdp'=4,'ctx'=4,'tp'=2] {'fsdp','ctx','tp'}, use_global_device_ids=true, to_apply=%region_17.18 | all-reduce | flops 4352 | bytes 34816 | tf_op jit(solution)/shard_map/psum | solution.py:311
  1139.4 440.9 %all-reduce.4.cloned.1.call-done = (bf16[512,3072]{0,1:T(8,128)(2,1)}, bf16[512,6144]{1,0:T(8,128)(2,1)}, bf16[256,2048]{1,0:T(8,128)(2,1)}, bf16[768,2048]{1,0:T(8,128)(2,1)}) async-done(((bf16[512,3072]{0,1:T(8,128)(2,1)}, bf16[512,6144]{1,0:T(8,128)(2,1)}, bf16[256,2048]{1,0:T(8,128)(2,1)}, bf16[768,2048]{1,0:T(8,128)(2,1)}), (bf16[512,3072]{0,1:T(8,128)(2,1)}, bf16[512,6144]{1,0:T(8,128)(2,1)}, ...) | async-done | bytes 13631504 | tf_op jit(solution)/shard_map/psum | solution.py:131
  (321 shorter events, 261.8 us)
Async XLA Ops:
  7.2 27.7 %all-gather.17.cloned.1.call-start = ((), (), s32[]{:S(2)}) async-start(), calls=%async_computation.12 | async-start | bytes 2621440 | tf_op jit(solution)/shard_map/all_gather | solution.py:88
  7.9 51.2 %all-gather.11.cloned.1.call-start = ((), (), s32[]{:S(2)}) async-start(), calls=%async_computation.9 | async-start | bytes 2621440 | tf_op jit(solution)/shard_map/all_gather | solution.py:88
  8.7 80.7 %all-gather.19.cloned.1.call-start = ((), (), s32[]{:S(2)}) async-start(), calls=%async_computation.13 | async-start | bytes 1310720 | tf_op jit(solution)/shard_map/all_gather | solution.py:202
  11.9 15.0 collective-permute-start
  37.9 86.7 %all-gather.15.cloned.1.call-start = ((), (), s32[]{:S(2)}) async-start(), calls=%async_computation.11 | async-start | bytes 5242880 | tf_op jit(solution)/shard_map/all_gather | solution.py:88
  38.5 118.0 %all-gather.13.cloned.1.call-start = ((), (), s32[]{:S(2)}) async-start(), calls=%async_computation.10 | async-start | bytes 1310720 | tf_op jit(solution)/shard_map/all_gather | solution.py:201
  64.2 126.5 %all-gather.21.cloned.1.call-start = ((), (), s32[]{:S(2)}) async-start(), calls=%async_computation.14 | async-start | bytes 5242880 | tf_op jit(solution)/shard_map/all_gather | solution.py:88
  64.8 162.0 %all-gather.23.cloned.1.call-start = ((), (), s32[]{:S(2)}) async-start(), calls=%async_computation.15 | async-start | bytes 5242880 | tf_op jit(solution)/shard_map/all_gather | solution.py:88
  65.5 186.3 %reduce-scatter.10.cloned.1.call-start = ((), (), s32[]{:S(2)}) async-start(), calls=%async_computation.16 | async-start | bytes 1572864 | tf_op jit(solution)/shard_map/reduce_scatter | solution.py:81
  231.2 104.2 %all-gather.25.cloned.1.call-start = ((), (), s32[]{:S(2)}) async-start(), calls=%async_computation.17 | async-start | bytes 15728640 | tf_op jit(solution)/shard_map/all_gather | solution.py:88
  232.0 187.0 %all-gather.27.cloned.1.call-start = ((), (), s32[]{:S(2)}) async-start(), calls=%async_computation.18 | async-start | bytes 15728640 | tf_op jit(solution)/shard_map/all_gather | solution.py:88
  232.6 270.1 %all-gather.29.cloned.1.call-start = ((), (), s32[]{:S(2)}) async-start(), calls=%async_computation.19 | async-start | bytes 15728640 | tf_op jit(solution)/shard_map/all_gather | solution.py:88
  233.3 320.0 %reduce-scatter.14.cloned.1.call-start = ((), (), s32[]{:S(2)}) async-start(), calls=%async_computation.21 | async-start | bytes 1572864 | tf_op jit(solution)/shard_map/reduce_scatter | solution.py:81
  256.3 14.9 collective-permute-start.1
  256.6 172.3 %collective-permute-start.2 = (bf16[128,2048]{1,0:T(8,128)(2,1)}, bf16[128,2048]{1,0:T(8,128)(2,1)}, u32[]{:S(2)}, u32[]{:S(2)}) collective-permute-start(bf16[128,2048]{1,0:T(8,128)(2,1)} %get-tuple-element.86), channel_id=1, source_target_pairs={{0,1},{1,0},{2,3},{3,2},{4,5},{5,4},{6,7},{7,6},{8,9},{9,8},{10,11... | collective-permute-start | bytes 1572872 | tf_op jit(solution)/shard_map/ppermute | solution.py:16
  532.7 105.3 %reduce-scatter.16.cloned.1.call-start = ((), (), s32[]{:S(2)}) async-start(), calls=%async_computation.22 | async-start | bytes 2621440 | tf_op jit(solution)/shard_map/reduce_scatter | solution.py:287
  557.4 13.6 collective-permute-start.3
  594.3 146.6 %reduce-scatter.22.cloned.1.call-start = ((), (), s32[]{:S(2)}) async-start(), calls=%async_computation.25 | async-start | bytes 5242880 | tf_op jit(solution)/shard_map/reduce_scatter | solution.py:114
  598.8 188.2 %reduce-scatter.26.cloned.1.call-start = ((), (), s32[]{:S(2)}) async-start(), calls=%async_computation.27 | async-start | bytes 15728640 | tf_op jit(solution)/shard_map/reduce_scatter | solution.py:114
  609.2 277.3 %reduce-scatter.20.cloned.1.call-start = ((), (), s32[]{:S(2)}) async-start(), calls=%async_computation.24 | async-start | bytes 15728640 | tf_op jit(solution)/shard_map/reduce_scatter | solution.py:114
  680.8 390.1 %reduce-scatter.24.cloned.1.call-start = ((), (), s32[]{:S(2)}) async-start(), calls=%async_computation.26 | async-start | bytes 31457280 | tf_op jit(solution)/shard_map/reduce_scatter | solution.py:114
  722.0 372.0 %reduce-scatter.18.cloned.1.call-start = ((), (), s32[]{:S(2)}) async-start(), calls=%async_computation.23 | async-start | bytes 1572864 | tf_op jit(solution)/shard_map/reduce_scatter | solution.py:81
  731.4 404.6 %reduce-scatter.12.cloned.1.call-start = ((), (), s32[]{:S(2)}) async-start(), calls=%async_computation.20 | async-start | bytes 1572864 | tf_op jit(solution)/shard_map/reduce_scatter | solution.py:81
  740.9 839.3 %all-reduce.4.cloned.1.call-start = ((), (), s32[]{:S(2)}) async-start(), calls=%async_computation.28 | async-start | bytes 27262976 | tf_op jit(solution)/shard_map/psum | solution.py:131
  (81 other events, 1168.9 us)
Sparse Core Ops, SparseCore 0:
  9.5 25.2 all-gather.16
  36.4 22.6 all-gather.10
  61.3 28.0 all-gather.18
  90.7 33.7 all-gather.14
  126.5 29.9 all-gather.12
  157.9 32.7 all-gather.20
  192.3 34.4 all-gather.22
  231.3 20.3 reduce-scatter.9
  253.3 82.0 all-gather.24
  336.8 82.0 all-gather.26
  420.5 82.0 all-gather.28
  532.8 20.3 reduce-scatter.13
  594.4 43.5 reduce-scatter.15
  641.0 43.7 reduce-scatter.21
  687.3 99.6 reduce-scatter.25
  789.4 97.1 reduce-scatter.19
  889.0 181.8 reduce-scatter.23
  1073.6 20.3 reduce-scatter.17
  1096.8 20.6 reduce-scatter.11
  1120.3 459.8 all-reduce.3
